TPU v7x, 256 devices: a whole 4x4x8 slice. The times are simulated.
256 devices in a mesh: dp: 8 (over z), seq: 32 (over y, x, core).
Axes of the slice: x: 4, y: 4, z: 8, core: 2. Of those that a mesh axis runs over, the one named last changes fastest.
Arguments:
- latents: bfloat16 [16, 16384, 1152], P('dp', 'seq'), may hold values from -56 to 56
- out_grad: bfloat16 [16, 16384, 1152], P('dp', 'seq'), may hold values from -6 to 6
- phrases: bfloat16 [16, 32, 1152], P('dp'), may hold values from -6 to 6
- query_weight: bfloat16 [1152, 1152], replicated, may hold values from -0.1875 to 0.1875
- key_weight: bfloat16 [1152, 1152], P('seq'), may hold values from -0.1875 to 0.1875
- value_weight: bfloat16 [1152, 1152], P('seq'), may hold values from -0.1875 to 0.1875
- first_weight: bfloat16 [1152, 1152], P('seq'), may hold values from -0.1875 to 0.1875
- second_weight: bfloat16 [1152, 1152], P('seq'), may hold values from -0.1875 to 0.1875
- region_first: int32 [16, 32], P('dp'), may hold values from 0 to 127, as said below
- region_last: int32 [16, 32], P('dp'), may hold values from 0 to 127
- phrase_counts: int32 [16], P('dp'), may hold values from 8 to 32, as said below
Outputs:
- latent_grad: bfloat16 [16, 16384, 1152], P('dp', 'seq')
- phrase_grad: bfloat16 [16, 32, 1152], P('dp')
- first_grad: float32 [1152, 1152], P('seq')
- second_grad: float32 [1152, 1152], P('seq')
Inputs may be any that keep to these rules, and one draw needn't show every extreme that they name: region_first <= region_last for every phrase; phrase 0 of every image covers all 128 blocks. Slots from phrase_counts on are padding.
All inputs are finite; a program needn't handle non-finite values.
Results may differ from a plain program's by a relative error of at most 0.015.
The roundings to bfloat16 on the way count: a program that leaves them out, or rounds other values in their place, can miss the bound.
Values may be sent and summed in bfloat16 or wider, within the bound.
A program may use at most 128 MiB of HBM per device.

v0:
```python
import jax
import jax.numpy as jnp
from jax import lax
from jax.sharding import PartitionSpec as P

H = 16


def silu_slope(pre_act):
    sigmoid = jax.nn.sigmoid(pre_act)
    return sigmoid * (1.0 + pre_act * (1.0 - sigmoid))


def times_transposed(left_arg, right_arg):
    return lax.dot_general(
        left_arg, right_arg, (((1,), (1,)), ((), ())), preferred_element_type=jnp.float32
    )


def transposed_times(left_arg, right_arg):
    return lax.dot_general(
        left_arg, right_arg, (((0,), (0,)), ((), ())), preferred_element_type=jnp.float32
    )


def attention_grads(
    latents,
    out_grad,
    query_weight,
    key_rows,
    value_rows,
    region_first,
    region_last,
    phrase_counts,
    offset,
):
    images, tokens, features = latents.shape
    slot_count = key_rows.shape[1]
    head_count = H
    head_size = features // head_count
    score_scale = head_size ** (-0.5)
    queries = jnp.dot(
        latents.reshape(images * tokens, features), query_weight, preferred_element_type=jnp.float32
    ).astype(jnp.bfloat16)
    query_heads = queries.reshape(images, tokens, head_count, head_size)
    key_heads = key_rows.reshape(images, slot_count, head_count, head_size)
    value_heads = value_rows.reshape(images, slot_count, head_count, head_size)
    grad_heads = out_grad.reshape(images, tokens, head_count, head_size)
    scores = (
        jnp.einsum("ithd,iphd->ithp", query_heads, key_heads, preferred_element_type=jnp.float32)
        * score_scale
    )
    block_ids = (offset + jnp.arange(tokens, dtype=jnp.int32)) // (tokens // 4)
    phrase_ids = jnp.arange(slot_count, dtype=jnp.int32)
    visible = (
        (phrase_ids[None, None, :] < phrase_counts[:, None, None])
        & (region_first[:, None, :] <= block_ids[None, :, None])
        & (block_ids[None, :, None] <= region_last[:, None, :])
    )
    scores = jnp.where(visible[:, :, None, :], scores, -jnp.inf)
    row_max = jnp.max(scores, axis=-1, keepdims=True)
    exponent = jnp.exp(scores - row_max)
    attn_probs = exponent / jnp.sum(exponent, axis=-1, keepdims=True)
    probs_low = attn_probs.astype(jnp.bfloat16)
    prob_grad = jnp.einsum(
        "ithd,iphd->ithp", grad_heads, value_heads, preferred_element_type=jnp.float32
    )
    inner_sum = jnp.sum(attn_probs * prob_grad, axis=-1, keepdims=True)
    score_grad = (attn_probs * (prob_grad - inner_sum) * score_scale).astype(jnp.bfloat16)
    query_grad = jnp.einsum(
        "ithp,iphd->ithd", score_grad, key_heads, preferred_element_type=jnp.float32
    ).astype(jnp.bfloat16)
    latent_grad = times_transposed(
        query_grad.reshape(images * tokens, features), query_weight
    ).astype(jnp.bfloat16)
    key_part = jnp.einsum(
        "ithp,ithd->iphd", score_grad, query_heads, preferred_element_type=jnp.float32
    ).reshape(images, slot_count, features)
    value_part = jnp.einsum(
        "ithp,ithd->iphd", probs_low, grad_heads, preferred_element_type=jnp.float32
    ).reshape(images, slot_count, features)
    return (latent_grad.reshape(images, tokens, features), key_part, value_part)


def local(
    latents,
    out_grad,
    phrases,
    query_weight,
    key_weight,
    value_weight,
    first_weight,
    second_weight,
    region_first,
    region_last,
    phrase_counts,
):
    images, tokens, features = latents.shape
    slot_count = phrases.shape[1]
    shard_rows = first_weight.shape[0]
    col_start = lax.axis_index("seq") * shard_rows
    phrase_rows = phrases.reshape(images * slot_count, features)

    def own_cols(matrix):
        return lax.dynamic_slice_in_dim(matrix, col_start, shard_rows, 1)

    full_first, full_second, full_key, full_value = (
        lax.all_gather(first_weight, "seq", axis=0, tiled=True),
        lax.all_gather(second_weight, "seq", axis=0, tiled=True),
        lax.all_gather(key_weight, "seq", axis=0, tiled=True),
        lax.all_gather(value_weight, "seq", axis=0, tiled=True),
    )
    pre_act = jnp.dot(phrase_rows, full_first, preferred_element_type=jnp.float32)
    hidden = jax.nn.silu(pre_act).astype(jnp.bfloat16)
    encoded = jnp.dot(hidden, full_second, preferred_element_type=jnp.float32).astype(jnp.bfloat16)
    key_rows = jnp.dot(encoded, full_key, preferred_element_type=jnp.float32).astype(jnp.bfloat16)
    value_rows = jnp.dot(encoded, full_value, preferred_element_type=jnp.float32).astype(
        jnp.bfloat16
    )
    offset = lax.axis_index("seq") * tokens
    latent_grad, key_part, value_part = attention_grads(
        latents,
        out_grad,
        query_weight,
        key_rows.reshape(images, slot_count, features),
        value_rows.reshape(images, slot_count, features),
        region_first,
        region_last,
        phrase_counts,
        offset,
    )
    key_sum_grad, value_sum_grad = lax.psum((key_part, value_part), "seq")
    key_grad = key_sum_grad.astype(jnp.bfloat16).reshape(images * slot_count, features)
    value_grad = value_sum_grad.astype(jnp.bfloat16).reshape(images * slot_count, features)
    encoded_grad = (
        times_transposed(key_grad, full_key) + times_transposed(value_grad, full_value)
    ).astype(jnp.bfloat16)
    second_grad = transposed_times(own_cols(hidden), encoded_grad)
    hidden_grad = times_transposed(encoded_grad, full_second)
    act_grad = (hidden_grad * silu_slope(pre_act)).astype(jnp.bfloat16)
    first_grad = transposed_times(own_cols(phrase_rows), act_grad)
    phrase_grad = times_transposed(act_grad, full_first).astype(jnp.bfloat16)
    first_grad, second_grad = lax.psum((first_grad, second_grad), "dp")
    return (latent_grad, phrase_grad.reshape(images, slot_count, features), first_grad, second_grad)


def solution(mesh):
    in_specs = (
        P("dp", "seq", None),
        P("dp", "seq", None),
        P("dp", None, None),
        P(),
        P("seq", None),
        P("seq", None),
        P("seq", None),
        P("seq", None),
        P("dp", None),
        P("dp", None),
        P("dp"),
    )
    out_specs = (P("dp", "seq", None), P("dp", None, None), P("seq", None), P("seq", None))
    return jax.shard_map(local, mesh=mesh, in_specs=in_specs, out_specs=out_specs, check_vma=False)
```

profile of v0, /device:TPU:4, one launch (start us, length us, event | category | flops | bytes accessed | tf_op | source)
XLA Modules:
  0.0 481.6 jit_solution(8142799292820077217)
XLA Ops:
  10.0 6.6 %convolution_convert_fusion.1 = bf16[1024,1152]{1,0:T(8,128)(2,1)} fusion(bf16[1024,1152]{1,0:T(8,128)(2,1)} %bitcast.91, bf16[1152,1152]{1,0:T(8,128)(2,1)S(1)} %copy-done), kind=kOutput, calls=%fused_computation.3 | convolution fusion | flops 2719088640 | bytes 7372800 | tf_op jit(solution)/shard_map/dot_general | solution.py:42
  16.6 9.6 %reshape.109 = bf16[2,512,16,72]{3,2,1,0:T(8,128)(2,1)} reshape(bf16[1024,1152]{1,0:T(8,128)(2,1)} %convolution_convert_fusion.1) | data formatting | bytes 4718592 | tf_op jit(solution)/shard_map/reshape | solution.py:45
  26.2 7.2 %copy.34 = bf16[2,512,16,72]{1,3,2,0:T(8,128)(2,1)} copy(bf16[2,512,16,72]{3,2,1,0:T(8,128)(2,1)} %reshape.109) | data formatting | bytes 4718592 | tf_op jit(solution)/shard_map/reshape | solution.py:45
  33.3 4.3 copy.35
  37.9 25.1 %all-gather.9.cloned.1.call-done = bf16[32,36,1152]{2,1,0:T(8,128)(2,1)} async-done(((bf16[1,36,1152]{2,1,0:T(8,128)(2,1)}), bf16[32,36,1152]{2,1,0:T(8,128)(2,1)}) %all-gather.9.cloned.1.call-update) | async-done | bytes 2654224 | tf_op jit(solution)/shard_map/all_gather | solution.py:108
  63.0 5.2 %reshape.102 = bf16[1152,1152]{1,0:T(8,128)(2,1)} reshape(bf16[32,36,1152]{2,1,0:T(8,128)(2,1)} %all-gather.9.cloned.1.call-done) | data formatting | bytes 5308416
  68.1 47.0 %all-gather.11.cloned.1.call-done = bf16[32,36,1152]{2,1,0:T(8,128)(2,1)} async-done(((bf16[1,36,1152]{2,1,0:T(8,128)(2,1)}), bf16[32,36,1152]{2,1,0:T(8,128)(2,1)}) %all-gather.11.cloned.1.call-update) | async-done | bytes 2654224 | tf_op jit(solution)/shard_map/all_gather | solution.py:109
  115.1 5.1 %reshape.104 = bf16[1152,1152]{1,0:T(8,128)(2,1)} reshape(bf16[32,36,1152]{2,1,0:T(8,128)(2,1)} %all-gather.11.cloned.1.call-done) | data formatting | bytes 5308416
  120.2 47.0 %all-gather.13.cloned.1.call-done = bf16[32,36,1152]{2,1,0:T(8,128)(2,1)} async-done(((bf16[1,36,1152]{2,1,0:T(8,128)(2,1)}), bf16[32,36,1152]{2,1,0:T(8,128)(2,1)}) %all-gather.13.cloned.1.call-update) | async-done | bytes 2654224 | tf_op jit(solution)/shard_map/all_gather | solution.py:110
  167.2 5.1 %reshape.106 = bf16[1152,1152]{1,0:T(8,128)(2,1)} reshape(bf16[32,36,1152]{2,1,0:T(8,128)(2,1)} %all-gather.13.cloned.1.call-done) | data formatting | bytes 5308416
  172.4 3.2 multiply_convert_fusion
  177.3 41.9 %all-gather.15.cloned.1.call-done = bf16[32,36,1152]{2,1,0:T(8,128)(2,1)} async-done(((bf16[1,36,1152]{2,1,0:T(8,128)(2,1)}), bf16[32,36,1152]{2,1,0:T(8,128)(2,1)}) %all-gather.15.cloned.1.call-update) | async-done | bytes 2654224 | tf_op jit(solution)/shard_map/all_gather | solution.py:111
  219.2 5.2 %reshape.108 = bf16[1152,1152]{1,0:T(8,128)(2,1)} reshape(bf16[32,36,1152]{2,1,0:T(8,128)(2,1)} %all-gather.15.cloned.1.call-done) | data formatting | bytes 5308416
  224.4 2.3 convolution_convert_fusion.3
  227.2 3.5 fusion.13
  230.8 4.0 fusion.33
  234.7 3.8 convolution_bitcast_fusion
  238.6 5.8 %convolution_bitcast_fusion.1 = f32[2,32,16,72]{3,1,2,0:T(8,128)} fusion(bf16[2,512,16,72]{1,3,2,0:T(8,128)(2,1)} %copy.34, f32[2,16,32,512]{3,2,1,0:T(8,128)} %fusion.13, f32[2,512,16,32]{1,3,2,0:T(8,128)} %get-tuple-element.11, f32[2,512,16]{1,2,0:T(8,128)S(1)} %get-tuple-element.10), kind=kOutput, calls=%fused_computation.22 | convolution fusion | flops 79183904 | bytes 6914048 | tf_op jit(solution)/shard_map/ithp,ithd->iphd/dot_general | solution.py:76
  244.4 5.9 %convert_bitcast_fusion = bf16[2,512,16,72]{1,3,2,0:T(8,128)(2,1)} fusion(f32[2,16,32,512]{3,2,1,0:T(8,128)} %fusion.13, bf16[2,32,16,72]{3,2,1,0:T(8,128)(2,1)S(1)} %reshape_reshape.6, f32[2,512,16,32]{1,3,2,0:T(8,128)} %get-tuple-element.11, f32[2,512,16]{1,2,0:T(8,128)S(1)} %get-tuple-element.10), kind=kOutput, calls=%fused_computation.6 | convolution fusion | flops 80363552 | bytes 6766592 | tf_op jit(solution)/shard_map/ithp,iphd->ithd/dot_general | solution.py:70
  254.2 123.2 %all-reduce.6 = (bf16[2,32,1152]{2,1,0:T(8,128)(2,1)S(1)}, bf16[2,32,1152]{2,1,0:T(8,128)(2,1)S(1)}) all-reduce(f32[2,32,1152]{2,1,0:T(8,128)S(1)} %reshape.96, f32[2,32,1152]{2,1,0:T(8,128)} %reshape.98), channel_id=1, replica_groups=mesh['dp'=8,'seq'=32] {'seq'}, use_global_device_ids=true, to_apply=%region_3.4 | all-reduce | flops 147456 | bytes 884736 | tf_op jit(solution)/shard_map/psum | solution.py:132
  377.4 2.8 fusion.38
  385.6 4.1 copy.38
  391.8 6.8 %convolution_convert_fusion = bf16[1024,1152]{1,0:T(8,128)(2,1)} fusion(bf16[1024,1152]{0,1:T(8,128)(2,1)} %bitcast.81, bf16[1152,1152]{1,0:T(8,128)(2,1)S(1)} %copy-done), kind=kOutput, calls=%fused_computation.2 | convolution fusion | flops 2719088640 | bytes 7372800 | tf_op jit(solution)/shard_map/dot_general | solution.py:15
  400.2 71.6 %all-reduce.5.cloned.1.call-done = (f32[36,1152]{1,0:T(8,128)}, f32[36,1152]{1,0:T(8,128)}) async-done(((f32[36,1152]{1,0:T(8,128)}, f32[36,1152]{1,0:T(8,128)}), (f32[36,1152]{1,0:T(8,128)}, f32[36,1152]{1,0:T(8,128)})) %all-reduce.5.cloned.1.call-update) | async-done | bytes 331792 | tf_op jit(solution)/shard_map/psum | solution.py:143
  (53 shorter events, 21.3 us)
Async XLA Ops:
  7.2 2.9 copy-start
  7.2 55.8 %all-gather.9.cloned.1.call-start = ((), (), s32[]{:S(2)}) async-start(), calls=%async_computation | async-start | bytes 3041280 | tf_op jit(solution)/shard_map/all_gather | solution.py:108
  7.9 107.2 %all-gather.11.cloned.1.call-start = ((), (), s32[]{:S(2)}) async-start(), calls=%async_computation.1 | async-start | bytes 3041280 | tf_op jit(solution)/shard_map/all_gather | solution.py:109
  8.7 158.6 %all-gather.13.cloned.1.call-start = ((), (), s32[]{:S(2)}) async-start(), calls=%async_computation.2 | async-start | bytes 3041280 | tf_op jit(solution)/shard_map/all_gather | solution.py:110
  9.4 209.8 %all-gather.15.cloned.1.call-start = ((), (), s32[]{:S(2)}) async-start(), calls=%async_computation.3 | async-start | bytes 3041280 | tf_op jit(solution)/shard_map/all_gather | solution.py:111
  10.0 461.8 %all-reduce.5.cloned.1.call-start = ((), (), s32[]{:S(2)}) async-start(), calls=%async_computation.4 | async-start | bytes 737280 | tf_op jit(solution)/shard_map/psum | solution.py:143
  33.3 4.3 copy-start.11
  33.3 4.4 copy-start.9
  33.3 4.4 copy-start.10
  120.2 52.1 %copy-start.8 = (bf16[2,32,1152]{2,1,0:T(8,128)(2,1)S(1)}, bf16[2,32,1152]{2,1,0:T(8,128)(2,1)}, u32[]{:S(2)}) copy-start(bf16[2,32,1152]{2,1,0:T(8,128)(2,1)} %param.13) | copy-start | bytes 442372
  172.4 3.2 copy-start.4
  172.4 3.9 copy-start.3
  175.6 0.7 copy-start.6
  377.4 2.8 copy-start.2
  380.3 2.7 copy-start.5
  380.3 2.7 copy-start.7
  391.8 6.8 %copy-start.1 = (bf16[1152,1152]{1,0:T(8,128)(2,1)S(1)}, bf16[1152,1152]{1,0:T(8,128)(2,1)}, u32[]{:S(2)}) copy-start(bf16[1152,1152]{1,0:T(8,128)(2,1)} %reshape.102) | copy-start | bytes 7962628
Sparse Core Ops, SparseCore 0:
  10.6 52.2 all-gather.8
  65.6 49.4 all-gather.10
  117.7 49.4 all-gather.12
  169.7 49.4 all-gather.14
  391.9 79.8 all-reduce.4
where the time goes:
time: 483 us; the launch traced here: 482 us
  waiting for transfers between devices  235 us (49%)
  blocking collectives  123 us (25%)
  local copies, waits for them, and re-layouts  56.1 us (12%)
  matrix products  52.9 us (11%)
  between operations  13.9 us (3%)
    psum x1, blocking collectives, local(): key_sum_grad, value_sum_grad = lax.psum((key_part, value_part), 'seq')  123 us
    psum x1, waiting for transfers between devices, local(): first_grad, second_grad = lax.psum((first_grad, second_grad), 'dp')  71.6 us
    all_gather x1, waiting for transfers between devices, local(): lax.all_gather(key_weight, 'seq', axis=0, tiled=True)  47 us
    all_gather x1, waiting for transfers between devices, local(): lax.all_gather(second_weight, 'seq', axis=0, tiled=True)  47 us
    all_gather x1, waiting for transfers between devices, local(): lax.all_gather(value_weight, 'seq', axis=0, tiled=True)  41.9 us
    unnamed x32, local copies, waits for them, and re-layouts  30.4 us
    all_gather x1, waiting for transfers between devices, local(): lax.all_gather(first_weight, 'seq', axis=0, tiled=True)  25.1 us
    reshape x2, local copies, waits for them, and re-layouts, attention_grads(): query_heads = queries.reshape(images, tokens, head_count, head_size)  16.7 us
  transfers between devices with their start and end apart: 5, of which 5 were waited for; matrix products, arithmetic and copies ran while one was open for 12% of the time, Pallas kernels for 0%

commit v1 on v0

v1 whole, which is shorter than its diff:
```python
import jax
import jax.numpy as jnp
from jax import lax
from jax.experimental import pallas as pl
from jax.experimental.pallas import tpu as pltpu
from jax.sharding import PartitionSpec as P

MESH = pl.DeviceIdType.MESH
BF16 = jnp.bfloat16
F32 = jnp.float32
D = 1152
HD = 72
NP = 32
NS = 32
NZ = 8
NJ = 9
CB = 128
SR = D // NS
SRP = 40
TOK = 512
WIN = 640
SCALE = HD ** (-0.5)


def dot_nn(a, b):
    return lax.dot_general(a, b, (((1,), (0,)), ((), ())), preferred_element_type=F32)


def dot_nt(a, b):
    return lax.dot_general(a, b, (((1,), (1,)), ((), ())), preferred_element_type=F32)


def dot_tn(a, b):
    return lax.dot_general(a, b, (((0,), (0,)), ((), ())), preferred_element_type=F32)


def cols(j):
    return pl.ds(pl.multiple_of(j * CB, CB), CB)


def kernel(
    first_ref, last_ref, count_ref,
    lat_hbm, og_hbm, wq_hbm, phr_ref, w1_ref, w2_ref, wk_ref, wv_ref,
    lg_hbm, pg_ref, fg_ref, sg_ref,
    x_s, g_s, wq_s, q_s, qg_s, l_s,
    wbuf, w_f32, wc,
    hid_src, hid_s, enc_s, kv_src, kv_s, pre_s,
    kbd_s, vbd_s, st_s, pt_s, pr_s, sg_s, kvp_s,
    b1_s, part_s, rs_s,
    eg_src, eg_s, ag_src, ag_s, pgsrc_s, pgf_s,
    hc_s, pc_s, gz_s, zr_s, zf_s,
    ld_sem, out_sem,
    wsend, wrecv, hsend, hrecv, esend, erecv, kvsend, kvrecv,
    b1send, b1recv, rssend, rsrecv, egsend, egrecv, agsend, agrecv, pgsend, pgrecv,
    zsend, zrecv, zasend, zarecv,
):
    d = lax.axis_index("dp")
    s = lax.axis_index("seq")
    my_i = s // 16
    my_j = lax.rem(s, 16)
    is_w = my_j < NJ
    w_refs = (w1_ref, w2_ref, wk_ref, wv_ref)

    def seq_of(i, j):
        return i * 16 + j

    def remote(src, dst, ssem, rsem, dd, ss):
        pltpu.make_async_remote_copy(
            src_ref=src, dst_ref=dst, send_sem=ssem, recv_sem=rsem,
            device_id=(dd, ss), device_id_type=MESH,
        ).start()

    def wait_bytes(ref, sem):
        pltpu.make_async_copy(ref, ref, sem).wait()

    loads = [
        pltpu.make_async_copy(lat_hbm, x_s, ld_sem.at[0]),
        pltpu.make_async_copy(wq_hbm, wq_s, ld_sem.at[1]),
        pltpu.make_async_copy(og_hbm, g_s, ld_sem.at[2]),
    ]
    for load in loads:
        load.start()

    barrier = pltpu.get_barrier_semaphore()

    def sig_seq(k, c):
        pl.semaphore_signal(barrier, inc=1, device_id=(d, lax.rem(s + k, NS)), device_id_type=MESH)
        return c

    def sig_dp(k, c):
        pl.semaphore_signal(barrier, inc=1, device_id=(lax.rem(d + k, NZ), s), device_id_type=MESH)
        return c

    lax.fori_loop(1, NS, sig_seq, 0)
    lax.fori_loop(1, NZ, sig_dp, 0)
    pl.semaphore_wait(barrier, NS - 1 + NZ - 1)

    for w in range(4):
        def send_w(n, c, w=w):
            t = seq_of(n // NJ, lax.rem(n, NJ))
            j = lax.rem(n, NJ)

            @pl.when(t != s)
            def _():
                remote(w_refs[w].at[:, cols(j)], wbuf.at[w, s], wsend.at[w], wrecv.at[w], d, t)

            return c

        lax.fori_loop(0, 2 * NJ, send_w, 0)

    @pl.when(is_w)
    def _():
        for w in range(4):
            wbuf[w, s] = w_refs[w][:, cols(my_j)]

    sel = (
        lax.broadcasted_iota(jnp.int32, (SRP, D), 1)
        == lax.broadcasted_iota(jnp.int32, (SRP, D), 0) + s * SR
    ) & (lax.broadcasted_iota(jnp.int32, (SRP, D), 0) < SR)
    sel = jnp.where(sel, 1.0, 0.0).astype(BF16)
    for i in range(2):
        pc_s[i] = dot_nt(sel, phr_ref[i]).astype(BF16)

    def q_proj(i):
        def body(n, c):
            w = pl.ds(pl.multiple_of(n * 384, 128), 384)
            q_s[i, :, w] = dot_nn(x_s[i], wq_s[:, w]).astype(BF16)
            return c

        lax.fori_loop(0, 3, body, 0)

    def compact(w):
        for p in range(NS):
            w_f32[p * SR : (p + 1) * SR, :] = wbuf[w, p].astype(F32)
        wc[w] = w_f32[...].astype(BF16)

    def to_co_workers(src, dst, ssem, rsem):
        def body(jj, c):
            @pl.when(jj != my_j)
            def _():
                remote(src, dst, ssem, rsem, d, seq_of(my_i, jj))

            return c

        lax.fori_loop(0, NJ, body, 0)

    def to_plane(src, dst, ssem, rsem):
        def body(k, c):
            remote(src, dst, ssem, rsem, d, lax.rem(s + k, NS))
            return c

        lax.fori_loop(1, NS, body, 0)

    loads[0].wait()
    loads[1].wait()
    q_proj(0)

    @pl.when(is_w)
    def _():
        wait_bytes(wbuf.at[0, pl.ds(0, NS - 1)], wrecv.at[0])
        compact(0)
        pre = dot_nn(phr_ref[my_i], wc[0])
        pre_s[...] = pre
        hid = (pre / (1.0 + jnp.exp(-pre))).astype(BF16)
        hid_src[...] = hid
        hid_s[my_i, :, cols(my_j)] = hid
        to_co_workers(hid_src, hid_s.at[my_i, :, cols(my_j)], hsend.at[0], hrecv.at[my_i])

    q_proj(1)

    @pl.when(is_w)
    def _():
        wait_bytes(wbuf.at[1, pl.ds(0, NS - 1)], wrecv.at[1])
        compact(1)
        wait_bytes(rs_s.at[0, pl.ds(0, NJ - 1), pl.ds(0, NP // 2)], hrecv.at[my_i])
        enc = dot_nn(hid_s[my_i], wc[1]).astype(BF16)
        enc_s[:, cols(my_j)] = enc
        to_co_workers(enc_s.at[:, cols(my_j)], enc_s.at[:, cols(my_j)], esend, erecv)

        def rest(k, c):
            t = lax.rem(s + k, NS)

            @pl.when((t // 16 != my_i) | (lax.rem(t, 16) >= NJ))
            def _():
                remote(hid_src, hid_s.at[my_i, :, cols(my_j)], hsend.at[1], hrecv.at[my_i], d, t)

            return c

        lax.fori_loop(1, NS, rest, 0)
        for w in (2, 3):
            wait_bytes(wbuf.at[w, pl.ds(0, NS - 1)], wrecv.at[w])
            compact(w)
        wait_bytes(rs_s.at[0, pl.ds(0, NJ - 1), pl.ds(0, NP // 2)], erecv)
        enc_all = enc_s[...]
        kv_src[0:NP] = dot_nn(enc_all, wc[2]).astype(BF16)
        kv_src[NP : 2 * NP] = dot_nn(enc_all, wc[3]).astype(BF16)
        kv_s[my_i, :, cols(my_j)] = kv_src[...]
        to_plane(kv_src, kv_s.at[my_i, :, cols(my_j)], kvsend, kvrecv.at[my_i])

    def wait_blocks(ref9, ref8, sem, i):
        mine = is_w & (my_i == i)

        @pl.when(mine)
        def _():
            wait_bytes(ref8, sem)

        @pl.when(jnp.logical_not(mine))
        def _():
            wait_bytes(ref9, sem)

    loads[2].wait()
    sub8 = lax.broadcasted_iota(jnp.int32, (8, WIN), 0)
    lane = lax.broadcasted_iota(jnp.int32, (8, WIN), 1)

    def attention(i):
        wait_blocks(
            b1_s.at[pl.ds(0, NJ), pl.ds(0, NP)], b1_s.at[pl.ds(0, NJ - 1), pl.ds(0, NP)],
            kvrecv.at[i], i,
        )
        for g in range(2):
            lo = 512 * g
            off = lane + (lo - 576 * g) - sub8 * HD
            own = jnp.where((off >= 0) & (off < HD), 1.0, 0.0)
            keys = kv_s[i, 0:NP, lo : lo + WIN].astype(F32)
            vals = kv_s[i, NP : 2 * NP, lo : lo + WIN].astype(F32)
            kbd_s[i, g] = (keys[:, None, :] * own[None]).reshape(8 * NP, WIN).astype(BF16)
            vbd_s[...] = (vals[:, None, :] * own[None]).reshape(8 * NP, WIN).astype(BF16)
            st_s[...] = dot_nt(kbd_s[i, g], q_s[i, :, lo : lo + WIN])
            pt_s[...] = dot_nt(vbd_s[...], g_s[i, :, lo : lo + WIN])

            def block(b, c):
                tok = cols(b)
                blk = s * 4 + b
                sc = []
                for p in range(NP):
                    vis = (p < count_ref[i]) & (first_ref[i, p] <= blk) & (blk <= last_ref[i, p])
                    sc.append(jnp.where(vis, st_s[8 * p : 8 * p + 8, tok] * SCALE, -jnp.inf))

                def tree(op, vals):
                    while len(vals) > 1:
                        vals = [op(*vals[k : k + 2]) if k + 1 < len(vals) else vals[k] for k in range(0, len(vals), 2)]
                    return vals[0]

                top = tree(jnp.maximum, sc)
                ex = [jnp.exp(v - top) for v in sc]
                inv = 1.0 / tree(jnp.add, ex)
                pr = [e * inv for e in ex]
                for p in range(0, NP, 2):
                    pr_s[8 * p : 8 * p + 16, tok] = jnp.concatenate([pr[p], pr[p + 1]], axis=0).astype(BF16)
                pg = [pt_s[8 * p : 8 * p + 8, tok] for p in range(NP)]
                inner = tree(jnp.add, [pr[p] * pg[p] for p in range(NP)])
                for p in range(0, NP, 2):
                    sg_s[i, g, 8 * p : 8 * p + 16, tok] = jnp.concatenate(
                        [pr[q] * (pg[q] - inner) * SCALE for q in (p, p + 1)], axis=0
                    ).astype(BF16)
                return c

            lax.fori_loop(0, 4, block, 0)
            kp = dot_nn(sg_s[i, g], q_s[i, :, lo : lo + WIN])
            vp = dot_nn(pr_s[...], g_s[i, :, lo : lo + WIN])
            kp = jnp.sum(kp.reshape(NP, 8, WIN) * own[None], axis=1)
            vp = jnp.sum(vp.reshape(NP, 8, WIN) * own[None], axis=1)
            both = jnp.concatenate([kp, vp], axis=0)
            if g == 0:
                kvp_s[i, :, 0:WIN] = both
            else:
                kvp_s[i, :, lo:WIN] = kvp_s[i, :, lo:WIN] + both[:, 0:CB]
                kvp_s[i, :, WIN:D] = both[:, CB:WIN]

        def send_part(jj, c):
            t = seq_of(i, jj)

            @pl.when(t != s)
            def _():
                remote(kvp_s.at[i, :, cols(jj)], b1_s.at[s], b1send, b1recv, d, t)

            return c

        lax.fori_loop(0, NJ, send_part, 0)

    for i in range(2):
        attention(i)

    def query_grad(i):
        a0 = dot_tn(sg_s[i, 0], kbd_s[i, 0])
        a1 = dot_tn(sg_s[i, 1], kbd_s[i, 1])
        qg_s[i, :, 0:512] = a0[:, 0:512].astype(BF16)
        qg_s[i, :, 512:WIN] = (a0[:, 512:WIN] + a1[:, 0:CB]).astype(BF16)
        qg_s[i, :, WIN:D] = a1[:, CB:WIN].astype(BF16)

    def latent(i):
        def body(n, c):
            w = pl.ds(pl.multiple_of(n * 384, 128), 384)
            l_s[i, :, w] = dot_nt(qg_s[i], wq_s[w, :]).astype(BF16)
            return c

        lax.fori_loop(0, 3, body, 0)
        pltpu.make_async_copy(l_s.at[i], lg_hbm.at[i], out_sem.at[i]).start()

    for i in range(2):
        query_grad(i)
    latent(0)

    for i in range(2):
        mine = is_w & (my_i == i)

        @pl.when(jnp.logical_not(mine))
        def _():
            wait_bytes(rs_s.at[0, :, pl.ds(0, NP // 2)], hrecv.at[i])

    for i in range(2):
        hc_s[i] = dot_nt(sel, hid_s[i]).astype(BF16)

    def scatter_sum(n):
        def body(jj, c):
            @pl.when(jj != my_j)
            def _():
                remote(
                    part_s.at[n, :, cols(jj)], rs_s.at[n, my_j], rssend.at[n], rsrecv.at[n],
                    d, seq_of(my_i, jj),
                )

            return c

        lax.fori_loop(0, NJ, body, 0)
        rs_s[n, my_j] = part_s[n, :, cols(my_j)]

    def scatter_wait(n):
        wait_bytes(rs_s.at[n, pl.ds(0, NJ - 1)], rsrecv.at[n])
        total = rs_s[n, 0]
        for k in range(1, NJ):
            total = total + rs_s[n, k]
        return total

    @pl.when(is_w)
    def _():
        b1_s[s] = kvp_s[my_i, :, cols(my_j)]
        wait_bytes(b1_s.at[pl.ds(0, NS - 1)], b1recv)
        total = b1_s[0]
        for k in range(1, NS):
            total = total + b1_s[k]
        low = total.astype(BF16)
        part_s[0] = dot_nt(low[0:NP], wc[2]) + dot_nt(low[NP : 2 * NP], wc[3])
        scatter_sum(0)

    latent(1)

    @pl.when(is_w)
    def _():
        eg = scatter_wait(0).astype(BF16)
        part_s[1] = dot_nt(eg, wc[1])
        scatter_sum(1)
        eg_src[...] = eg
        eg_s[my_i, :, cols(my_j)] = eg
        to_plane(eg_src, eg_s.at[my_i, :, cols(my_j)], egsend, egrecv.at[my_i])
        hg = scatter_wait(1)
        pre = pre_s[...]
        sig = 1.0 / (1.0 + jnp.exp(-pre))
        ag = (hg * (sig * (1.0 + pre * (1.0 - sig)))).astype(BF16)
        ag_src[...] = ag
        ag_s[my_i, :, cols(my_j)] = ag
        to_plane(ag_src, ag_s.at[my_i, :, cols(my_j)], agsend, agrecv.at[my_i])
        part_s[2] = dot_nt(ag, wc[0])
        scatter_sum(2)

    def own8(n):
        return lax.rem(s, NZ)

    def z_scatter(k):
        def body(b, c):
            owner = jnp.where(b < NZ, b, own8(k))

            @pl.when(owner != d)
            def _():
                remote(gz_s.at[k, :, cols(b)], zr_s.at[k, b // NZ, d], zsend.at[k], zrecv.at[k, b // NZ], owner, s)

            return c

        lax.fori_loop(0, NJ, body, 0)
        zr_s[k, 0, d] = gz_s[k, :, cols(d)]

        @pl.when(own8(k) == d)
        def _():
            zr_s[k, 1, d] = gz_s[k, :, NZ * CB : D]

    def z_gather(k):
        def reduce(h, b):
            wait_bytes(zr_s.at[k, h, pl.ds(0, NZ - 1)], zrecv.at[k, h])
            total = zr_s[k, h, 0]
            for n in range(1, NZ):
                total = total + zr_s[k, h, n]
            zf_s[k, :, cols(b)] = total

            def body(n, c):
                remote(zf_s.at[k, :, cols(b)], zf_s.at[k, :, cols(b)], zasend.at[k, h], zarecv.at[k], lax.rem(d + n, NZ), s)
                return c

            lax.fori_loop(1, NZ, body, 0)

        reduce(0, d)

        @pl.when(own8(k) == d)
        def _():
            reduce(1, NZ)

    def z_finish(k, out):
        @pl.when(own8(k) == d)
        def _():
            wait_bytes(zr_s.at[k, 0, pl.ds(0, NZ - 1)], zarecv.at[k])

        @pl.when(own8(k) != d)
        def _():
            wait_bytes(zr_s.at[k, 0], zarecv.at[k])

        out[...] = zf_s[k, 0:SR, :]

    for i in range(2):
        wait_blocks(
            rs_s.at[0, :, pl.ds(0, NP // 2)], rs_s.at[0, pl.ds(0, NJ - 1), pl.ds(0, NP // 2)], egrecv.at[i], i
        )
    gz_s[0] = dot_nn(hc_s[0], eg_s[0]) + dot_nn(hc_s[1], eg_s[1])
    z_scatter(0)

    for i in range(2):
        wait_blocks(
            rs_s.at[0, :, pl.ds(0, NP // 2)], rs_s.at[0, pl.ds(0, NJ - 1), pl.ds(0, NP // 2)], agrecv.at[i], i
        )
    gz_s[1] = dot_nn(pc_s[0], ag_s[0]) + dot_nn(pc_s[1], ag_s[1])
    z_scatter(1)
    z_gather(0)

    @pl.when(is_w)
    def _():
        pgsrc_s[...] = scatter_wait(2).astype(BF16)
        pgf_s[my_i, :, cols(my_j)] = pgsrc_s[...]
        to_plane(pgsrc_s, pgf_s.at[my_i, :, cols(my_j)], pgsend, pgrecv.at[my_i])

    z_gather(1)
    z_finish(0, sg_ref)
    for i in range(2):
        wait_blocks(
            rs_s.at[0, :, pl.ds(0, NP // 2)], rs_s.at[0, pl.ds(0, NJ - 1), pl.ds(0, NP // 2)], pgrecv.at[i], i
        )
    pg_ref[...] = pgf_s[...]
    z_finish(1, fg_ref)

    for i in range(2):
        pltpu.make_async_copy(l_s.at[i], lg_hbm.at[i], out_sem.at[i]).wait()
    for w in range(4):
        @pl.when(is_w)
        def _():
            wait_bytes(wbuf.at[w, pl.ds(0, 2 * NJ - 1)], wsend.at[w])

        @pl.when(jnp.logical_not(is_w))
        def _():
            wait_bytes(wbuf.at[w, pl.ds(0, 2 * NJ)], wsend.at[w])

    @pl.when(is_w)
    def _():
        wait_bytes(b1_s.at[pl.ds(0, 2 * NJ - 1)], b1send)
        wait_bytes(rs_s.at[0, pl.ds(0, NJ - 1), pl.ds(0, NP // 2)], hsend.at[0])
        wait_bytes(b1_s.at[pl.ds(0, NS - NJ), pl.ds(0, NP // 2)], hsend.at[1])
        wait_bytes(rs_s.at[0, pl.ds(0, NJ - 1), pl.ds(0, NP // 2)], esend)
        wait_bytes(b1_s.at[pl.ds(0, NS - 1), pl.ds(0, NP)], kvsend)
        for n in range(3):
            wait_bytes(rs_s.at[n, pl.ds(0, NJ - 1)], rssend.at[n])
        for sem in (egsend, agsend, pgsend):
            wait_bytes(b1_s.at[pl.ds(0, NS - 1), pl.ds(0, NP // 2)], sem)

    @pl.when(jnp.logical_not(is_w))
    def _():
        wait_bytes(b1_s.at[pl.ds(0, 2 * NJ)], b1send)

    for k in range(2):
        @pl.when(own8(k) == d)
        def _():
            wait_bytes(zr_s.at[k, 0, pl.ds(0, NZ - 1)], zsend.at[k])
            wait_bytes(zr_s.at[k, 0, pl.ds(0, NZ - 1)], zasend.at[k, 1])

        @pl.when(own8(k) != d)
        def _():
            wait_bytes(zr_s.at[k, 0], zsend.at[k])

        wait_bytes(zr_s.at[k, 0, pl.ds(0, NZ - 1)], zasend.at[k, 0])


def local(
    latents, out_grad, phrases, query_weight, key_weight, value_weight, first_weight, second_weight,
    region_first, region_last, phrase_counts,
):
    vmem = pl.BlockSpec(memory_space=pltpu.VMEM)
    smem = pl.BlockSpec(memory_space=pltpu.SMEM)
    anyspace = pl.BlockSpec(memory_space=pl.ANY)
    V = pltpu.VMEM
    DMA = pltpu.SemaphoreType.DMA
    scratch = [
        V((2, TOK, D), BF16), V((2, TOK, D), BF16), V((D, D), BF16), V((2, TOK, D), BF16), V((2, TOK, D), BF16),
        V((2, TOK, D), BF16),
        V((4, NS, SR, CB), BF16), V((D, CB), F32), V((4, D, CB), BF16),
        V((NP, CB), BF16), V((2, NP, D), BF16), V((NP, D), BF16), V((2 * NP, CB), BF16), V((2, 2 * NP, D), BF16),
        V((NP, CB), F32),
        V((2, 2, 8 * NP, WIN), BF16), V((8 * NP, WIN), BF16), V((8 * NP, TOK), F32), V((8 * NP, TOK), F32),
        V((8 * NP, TOK), BF16), V((2, 2, 8 * NP, TOK), BF16), V((2, 2 * NP, D), F32),
        V((NS, 2 * NP, CB), F32), V((3, NP, D), F32), V((3, NJ, NP, CB), F32),
        V((NP, CB), BF16), V((2, NP, D), BF16), V((NP, CB), BF16), V((2, NP, D), BF16), V((NP, CB), BF16),
        V((2, NP, D), BF16),
        V((2, SRP, NP), BF16), V((2, SRP, NP), BF16), V((2, SRP, D), F32), V((2, 2, NZ, SRP, CB), F32),
        V((2, SRP, D), F32),
        DMA((3,)), DMA((2,)),
        DMA((4,)), DMA((4,)), DMA((2,)), DMA((2,)), DMA(()), DMA(()), DMA(()), DMA((2,)),
        DMA(()), DMA(()), DMA((3,)), DMA((3,)), DMA(()), DMA((2,)), DMA(()), DMA((2,)), DMA(()), DMA((2,)),
        DMA((2,)), DMA((2, 2)), DMA((2, 2)), DMA((2,)),
    ]
    return pl.pallas_call(
        kernel,
        out_shape=(
            jax.ShapeDtypeStruct((2, TOK, D), BF16),
            jax.ShapeDtypeStruct((2, NP, D), BF16),
            jax.ShapeDtypeStruct((SR, D), F32),
            jax.ShapeDtypeStruct((SR, D), F32),
        ),
        in_specs=[smem] * 3 + [anyspace] * 3 + [vmem] * 5,
        out_specs=(anyspace, vmem, vmem, vmem),
        scratch_shapes=scratch,
        compiler_params=pltpu.CompilerParams(
            collective_id=0, has_side_effects=True, vmem_limit_bytes=48 * 2**20
        ),
    )(
        region_first, region_last, phrase_counts, latents, out_grad, query_weight, phrases,
        first_weight, second_weight, key_weight, value_weight,
    )


def solution(mesh):
    in_specs = (
        P("dp", "seq", None), P("dp", "seq", None), P("dp", None, None), P(),
        P("seq", None), P("seq", None), P("seq", None), P("seq", None),
        P("dp", None), P("dp", None), P("dp"),
    )
    out_specs = (P("dp", "seq", None), P("dp", None, None), P("seq", None), P("seq", None))
    return jax.shard_map(local, mesh=mesh, in_specs=in_specs, out_specs=out_specs, check_vma=False)
```

time: 483 us -> 107 us (0.22)
  waiting for transfers between devices: 235 us -> 0 us
  blocking collectives: 123 us -> 0 us
  Pallas kernels: 0 us -> 94.5 us
  matrix products: 52.9 us -> 0 us
  local copies, waits for them, and re-layouts: 56.1 us -> 11.6 us
  between operations: 13.9 us -> 0.66 us
    all_gather x4 -> x0, waiting for transfers between devices: 161 us -> none  [the longest x1 47 us: local(): lax.all_gather(key_weight, 'seq', axis=0, tiled=True)]
    psum x1 -> x0, blocking collectives: 123 us -> none  [local(): key_sum_grad, value_sum_grad = lax.psum((key_part, value_part), 'seq')]
    pallas_call x0 -> x1, Pallas kernels: none -> 94.5 us  [local(): pl.pallas_call(kernel, out_shape=(jax.ShapeDtypeStruct((2, TOK, D), BF16)...]
    psum x1 -> x0, waiting for transfers between devices: 71.6 us -> none  [local(): first_grad, second_grad = lax.psum((first_grad, second_grad), 'dp')]
    dot_general x16 -> x0, matrix products: 48.9 us -> none  [the longest x5 13.1 us: times_transposed(): lax.dot_general(left_arg, right_arg, (((1,), (1,)), ((), ())), preferred_...]
    unnamed x32 -> x22, local copies, waits for them, and re-layouts: 30.4 us -> 11.6 us
    reshape x4 -> x0, local copies, waits for them, and re-layouts: 17.9 us -> none  [the longest x2 16.7 us: attention_grads(): query_heads = queries.reshape(images, tokens, head_count, head_size)]
  transfers between devices with their start and end apart: 5 -> 0, of which waited for: 5 -> 0; matrix products, arithmetic and copies ran while one was open for 12% -> 0% of each run, Pallas kernels for 0% -> 0%
where the time goes in v1:
time: 107 us
  Pallas kernels  94.5 us (88%)
  local copies, waits for them, and re-layouts  11.6 us (11%)
    pallas_call x1, Pallas kernels, local(): pl.pallas_call(kernel, out_shape=(jax.ShapeDtypeStruct((2, TOK, D), BF16)...  94.5 us
    unnamed x22, local copies, waits for them, and re-layouts  11.6 us

profile of v1, /device:TPU:4, one launch (start us, length us, event | category | flops | bytes accessed | tf_op | source)
XLA Modules:
  0.0 106.7 jit_solution(17624105200408721311)
XLA Ops:
  0.6 0.0 copy-start
  0.6 1.7 %copy-done = bf16[2,512,1152]{2,1,0:T(8,128)(2,1)S(1)} copy-done((bf16[2,512,1152]{2,1,0:T(8,128)(2,1)S(1)}, bf16[2,512,1152]{2,1,0:T(8,128)(2,1)}, u32[]{:S(2)}) %copy-start) | copy-done | bytes 2359320
  2.3 0.0 copy-start.1
  2.3 0.9 copy-done.1
  3.2 0.0 copy-start.2
  3.2 0.9 copy-done.2
  4.1 0.0 copy-start.3
  4.1 0.9 copy-done.3
  5.0 0.0 copy-start.4
  5.0 0.9 copy-done.4
  5.9 0.0 copy-start.5
  5.9 0.9 copy-done.5
  6.8 0.0 copy-start.6
  6.8 0.7 copy-done.6
  7.5 0.0 copy-start.7
  7.5 0.7 copy-done.7
  8.1 0.0 copy-start.8
  8.1 0.7 copy-done.8
  8.8 94.5 %shard_map.138 = (bf16[2,512,1152]{2,1,0:T(8,128)(2,1)S(1)}, bf16[2,32,1152]{2,1,0:T(8,128)(2,1)S(1)}, f32[36,1152]{1,0:T(8,128)S(1)}, f32[36,1152]{1,0:T(8,128)S(1)}) custom-call(s32[2,32]{1,0:T(2,128)S(1)} %copy-done.6, s32[2,32]{1,0:T(2,128)S(1)} %copy-done.7, s32[2]{0:T(128)S(1)} %copy-done.8, bf16[2,512,1152]{2,1,0:T(8,128)(2,1)S(1)} %copy-done, ...), custom_call_target="tpu_custom_call" | custom-call | tf_op jit(solution)/shard_map/pallas_call | solution.py:514
  103.3 1.4 %copy.19 = bf16[2,512,1152]{2,1,0:T(8,128)(2,1)} copy(bf16[2,512,1152]{2,1,0:T(8,128)(2,1)S(1)} %get-tuple-element.8) | data formatting | bytes 4718592
  104.7 0.7 copy.20
  105.4 0.7 copy.21
  106.1 0.7 copy.22
Async XLA Ops:
  0.6 1.7 %copy-start = (bf16[2,512,1152]{2,1,0:T(8,128)(2,1)S(1)}, bf16[2,512,1152]{2,1,0:T(8,128)(2,1)}, u32[]{:S(2)}) copy-start(bf16[2,512,1152]{2,1,0:T(8,128)(2,1)} %lat_hbm.1) | copy-start | bytes 7077892
  2.3 0.9 copy-start.1
  3.2 0.9 copy-start.2
  4.1 0.9 copy-start.3
  5.0 0.9 copy-start.4
  5.9 0.9 copy-start.5
  6.8 0.7 copy-start.6
  7.5 0.7 copy-start.7
  8.1 0.7 copy-start.8

commit v2 on v1

v2 whole, which is shorter than its diff:
```python
import jax
import jax.numpy as jnp
from jax import lax
from jax.experimental import pallas as pl
from jax.experimental.pallas import tpu as pltpu
from jax.sharding import PartitionSpec as P

MESH = pl.DeviceIdType.MESH
BF16 = jnp.bfloat16
F32 = jnp.float32
D = 1152
HD = 72
NP = 32
NS = 32
NZ = 8
NJ = 9
CB = 128
SR = D // NS
SRP = 40
TOK = 512
WIN = 640
SCALE = HD ** (-0.5)


def dot_nn(a, b):
    return lax.dot_general(a, b, (((1,), (0,)), ((), ())), preferred_element_type=F32)


def dot_nt(a, b):
    return lax.dot_general(a, b, (((1,), (1,)), ((), ())), preferred_element_type=F32)


def dot_tn(a, b):
    return lax.dot_general(a, b, (((0,), (0,)), ((), ())), preferred_element_type=F32)


def cols(j):
    return pl.ds(pl.multiple_of(j * CB, CB), CB)


def where_worker(n):
    i, j = n // NJ, lax.rem(n, NJ)
    k = j // 2
    y = lax.rem(1 + 2 * i + jnp.where(k == 1, 3, jnp.where(k == 2, 1, 0)), 4)
    x = lax.rem(1 + 2 * i + jnp.where(k == 3, 3, jnp.where(k == 4, 1, 0)), 4)
    return (y * 4 + x) * 2 + lax.rem(j, 2)


def worker_at(t):
    y, x, c = t // 8, lax.rem(t // 2, 4), lax.rem(t, 2)

    def block(i):
        ry, rx = lax.rem(y + 7 - 2 * i, 4), lax.rem(x + 7 - 2 * i, 4)
        row = jnp.where(rx == 0, 0, jnp.where(rx == 3, 3, jnp.where(rx == 1, 4, 9)))
        col = jnp.where(ry == 3, 1, jnp.where(ry == 1, 2, 9))
        k = jnp.where(ry == 0, row, jnp.where(rx == 0, col, 9))
        return 2 * k + c

    j0, j1 = block(0), block(1)
    i = jnp.where(j0 < NJ, 0, 1)
    j = jnp.where(j0 < NJ, j0, j1)
    return i, j, j < NJ


def kernel(
    first_hbm, last_hbm, count_hbm,
    lat_hbm, og_hbm, wq_hbm, phr_hbm, w1_hbm, w2_hbm, wk_hbm, wv_hbm,
    l_ref, pg_ref, fg_ref, sg_ref,
    first_ref, last_ref, count_ref, phr_ref, w_s,
    x_s, g_s, wq_s, q_s, qg_s,
    wbuf, w_f32, wc,
    hid_src, hid_s, enc_s, kv_src, kv_s, pre_s,
    kbd_s, vbd_s, st_s, pt_s, pr_s, sg_s, kvp_s, pair_s,
    kvb_s, b1_s, part_s, rs_s,
    eg_src, eg_s, ag_src, ag_s, pgsrc_s, pgf_s,
    hc_s, pc_s, gz_s, zr_s, zf_s,
    ld_sem,
    wsend, wrecv, hsend, hrecv, esend, erecv, kvsend, kvrecv, fwsend, fwrecv, prsend, prrecv,
    b1send, b1recv, rssend, rsrecv, egsend, egrecv, agsend, agrecv, pgsend, pgrecv,
    zsend, zrecv, zasend, zarecv,
):
    d = lax.axis_index("dp")
    s = lax.axis_index("seq")
    chip, core = s // 2, lax.rem(s, 2)
    other = 1 - core
    mate = s + 1 - 2 * core
    my_i, my_j, is_w = worker_at(s)
    my_j = jnp.where(is_w, my_j, 0)

    def remote(src, dst, ssem, rsem, dd, ss):
        pltpu.make_async_remote_copy(
            src_ref=src, dst_ref=dst, send_sem=ssem, recv_sem=rsem,
            device_id=(dd, ss), device_id_type=MESH,
        ).start()

    def wait_bytes(ref, sem):
        pltpu.make_async_copy(ref, ref, sem).wait()

    barrier = pltpu.get_barrier_semaphore()

    def sig_seq(k, c):
        pl.semaphore_signal(barrier, inc=1, device_id=(d, lax.rem(s + k, NS)), device_id_type=MESH)
        return c

    def sig_dp(k, c):
        pl.semaphore_signal(barrier, inc=1, device_id=(lax.rem(d + k, NZ), s), device_id_type=MESH)
        return c

    lax.fori_loop(1, NS, sig_seq, 0)
    lax.fori_loop(1, NZ, sig_dp, 0)

    pairs = (
        (w1_hbm, w_s.at[0]), (w2_hbm, w_s.at[1]), (wk_hbm, w_s.at[2]), (wv_hbm, w_s.at[3]),
        (lat_hbm, x_s), (wq_hbm, wq_s), (phr_hbm, phr_ref), (og_hbm, g_s),
        (first_hbm, first_ref), (last_hbm, last_ref), (count_hbm, count_ref),
    )
    loads = [pltpu.make_async_copy(a, b, ld_sem.at[n]) for n, (a, b) in enumerate(pairs)]
    for load in loads:
        load.start()

    def q_proj(i):
        q_s[i] = dot_nn(x_s[i], wq_s[...]).astype(BF16)

    loads[4].wait()
    loads[5].wait()
    q_proj(0)
    for n in range(4):
        loads[n].wait()
    pl.semaphore_wait(barrier, NS - 1 + NZ - 1)

    def send_weight(w):
        def body(k, c):
            n = lax.rem(s + k, 2 * NJ)
            j = lax.rem(n, NJ)
            t = where_worker(n)

            @pl.when(t != s)
            def _():
                remote(w_s.at[w, :, cols(j)], wbuf.at[w, s], wsend.at[w], wrecv.at[w], d, t)

            return c

        lax.fori_loop(0, 2 * NJ, body, 0)

    send_weight(0)
    send_weight(1)

    @pl.when(is_w)
    def _():
        for w in range(4):
            wbuf[w, s] = w_s[w, :, cols(my_j)]

    loads[6].wait()
    sel = (
        lax.broadcasted_iota(jnp.int32, (SRP, D), 1)
        == lax.broadcasted_iota(jnp.int32, (SRP, D), 0) + s * SR
    ) & (lax.broadcasted_iota(jnp.int32, (SRP, D), 0) < SR)
    sel = jnp.where(sel, 1.0, 0.0).astype(BF16)
    for i in range(2):
        pc_s[i] = dot_nt(sel, phr_ref[i]).astype(BF16)
    q_proj(1)

    @pl.when(jnp.logical_not(is_w))
    def _():
        send_weight(2)
        send_weight(3)

    def compact(w):
        for p in range(NS):
            w_f32[p * SR : (p + 1) * SR, :] = wbuf[w, p].astype(F32)
        wc[w] = w_f32[...].astype(BF16)

    def to_co_workers(src, dst, ssem, rsem):
        def body(k, c):
            jj = lax.rem(my_j + k, NJ)
            remote(src, dst, ssem, rsem, d, where_worker(my_i * NJ + jj))
            return c

        lax.fori_loop(1, NJ, body, 0)

    def to_plane(src, dst, ssem, rsem):
        def body(k, c):
            remote(src, dst, ssem, rsem, d, lax.rem(s + k, NS))
            return c

        lax.fori_loop(1, NS, body, 0)

    def slabs_of(n):
        return rs_s.at[0, pl.ds(0, n), pl.ds(0, NP // 2)]

    def wide_s(n):
        return wc.at[0, pl.ds(0, n * NP)]

    @pl.when(is_w)
    def _():
        wait_bytes(wbuf.at[0, pl.ds(0, NS - 1)], wrecv.at[0])
        compact(0)
        pre = dot_nn(phr_ref[my_i], wc[0])
        pre_s[...] = pre
        hid = (pre / (1.0 + jnp.exp(-pre))).astype(BF16)
        hid_src[...] = hid
        hid_s[my_i, :, cols(my_j)] = hid
        to_co_workers(hid_src, hid_s.at[my_i, :, cols(my_j)], hsend.at[0], hrecv.at[my_i])
        send_weight(2)
        send_weight(3)
        wait_bytes(wbuf.at[1, pl.ds(0, NS - 1)], wrecv.at[1])
        compact(1)
        wait_bytes(slabs_of(NJ - 1), hrecv.at[my_i])
        enc = dot_nn(hid_s[my_i], wc[1]).astype(BF16)
        enc_s[:, cols(my_j)] = enc
        to_co_workers(enc_s.at[:, cols(my_j)], enc_s.at[:, cols(my_j)], esend, erecv)
        for w in (2, 3):
            wait_bytes(wbuf.at[w, pl.ds(0, NS - 1)], wrecv.at[w])
            compact(w)
        wait_bytes(slabs_of(NJ - 1), erecv)
        enc_all = enc_s[...]
        kv_src[0:NP] = dot_nn(enc_all, wc[2]).astype(BF16)
        kv_src[NP : 2 * NP] = dot_nn(enc_all, wc[3]).astype(BF16)

        def send_kv(k, c):
            t = 2 * lax.rem(chip + k, NS // 2) + my_i

            @pl.when(t != s)
            def _():
                remote(kv_src, kv_s.at[my_i, :, cols(my_j)], kvsend, kvrecv, d, t)

            return c

        lax.fori_loop(0, NS // 2, send_kv, 0)

        @pl.when(core == my_i)
        def _():
            kv_s[my_i, :, cols(my_j)] = kv_src[...]

        def rest(k, c):
            t = lax.rem(s + k, NS)
            ti, _, tw = worker_at(t)

            @pl.when(jnp.logical_not(tw) | (ti != my_i))
            def _():
                remote(hid_src, hid_s.at[my_i, :, cols(my_j)], hsend.at[1], hrecv.at[my_i], d, t)

            return c

        lax.fori_loop(1, NS, rest, 0)

    for n in range(7, 11):
        loads[n].wait()
    sub8 = lax.broadcasted_iota(jnp.int32, (8, WIN), 0)
    lane = lax.broadcasted_iota(jnp.int32, (8, WIN), 1)

    def attention(i):
        for g in range(2):
            lo = 512 * g
            off = lane + (lo - 576 * g) - sub8 * HD
            own = jnp.where((off >= 0) & (off < HD), 1.0, 0.0)
            keys = kv_s[i, 0:NP, lo : lo + WIN].astype(F32)
            vals = kv_s[i, NP : 2 * NP, lo : lo + WIN].astype(F32)
            kbd_s[i, g] = (keys[:, None, :] * own[None]).reshape(8 * NP, WIN).astype(BF16)
            vbd_s[...] = (vals[:, None, :] * own[None]).reshape(8 * NP, WIN).astype(BF16)
            st_s[...] = dot_nt(kbd_s[i, g], q_s[i, :, lo : lo + WIN])
            pt_s[...] = dot_nt(vbd_s[...], g_s[i, :, lo : lo + WIN])

            def block(b, c):
                tok = cols(b)
                blk = s * 4 + b
                sc = []
                for p in range(NP):
                    vis = (p < count_ref[i]) & (first_ref[i, p] <= blk) & (blk <= last_ref[i, p])
                    sc.append(jnp.where(vis, st_s[8 * p : 8 * p + 8, tok] * SCALE, -jnp.inf))

                def tree(op, vals):
                    while len(vals) > 1:
                        vals = [op(*vals[k : k + 2]) if k + 1 < len(vals) else vals[k] for k in range(0, len(vals), 2)]
                    return vals[0]

                top = tree(jnp.maximum, sc)
                ex = [jnp.exp(v - top) for v in sc]
                inv = 1.0 / tree(jnp.add, ex)
                pr = [e * inv for e in ex]
                for p in range(0, NP, 2):
                    pr_s[8 * p : 8 * p + 16, tok] = jnp.concatenate([pr[p], pr[p + 1]], axis=0).astype(BF16)
                pg = [pt_s[8 * p : 8 * p + 8, tok] for p in range(NP)]
                inner = tree(jnp.add, [pr[p] * pg[p] for p in range(NP)])
                for p in range(0, NP, 2):
                    sg_s[i, g, 8 * p : 8 * p + 16, tok] = jnp.concatenate(
                        [pr[q] * (pg[q] - inner) * SCALE for q in (p, p + 1)], axis=0
                    ).astype(BF16)
                return c

            lax.fori_loop(0, 4, block, 0)
            kp = dot_nn(sg_s[i, g], q_s[i, :, lo : lo + WIN])
            vp = dot_nn(pr_s[...], g_s[i, :, lo : lo + WIN])
            kp = jnp.sum(kp.reshape(NP, 8, WIN) * own[None], axis=1)
            vp = jnp.sum(vp.reshape(NP, 8, WIN) * own[None], axis=1)
            both = jnp.concatenate([kp, vp], axis=0)
            if g == 0:
                kvp_s[i, :, 0:WIN] = both
            else:
                kvp_s[i, :, lo:WIN] = kvp_s[i, :, lo:WIN] + both[:, 0:CB]
                kvp_s[i, :, WIN:D] = both[:, CB:WIN]

    direct = is_w & (my_i == core)

    @pl.when(direct)
    def _():
        wait_bytes(b1_s.at[pl.ds(0, NJ - 1)], kvrecv)

    @pl.when(jnp.logical_not(direct))
    def _():
        wait_bytes(b1_s.at[pl.ds(0, NJ)], kvrecv)

    remote(kv_s.at[core], kv_s.at[core], fwsend, fwrecv, d, mate)
    attention(core)
    remote(kvp_s.at[core], pair_s, prsend, prrecv, d, mate)
    wait_bytes(kv_s.at[other], fwrecv)
    attention(other)
    wait_bytes(pair_s, prrecv)
    kvb_s[...] = (kvp_s[other] + pair_s[...]).astype(BF16)

    def send_part(k, c):
        jj = lax.rem(chip + k, NJ)
        t = where_worker(other * NJ + jj)

        @pl.when(t != s)
        def _():
            remote(kvb_s.at[:, cols(jj)], b1_s.at[chip], b1send, b1recv, d, t)

        return c

    lax.fori_loop(0, NJ, send_part, 0)
    from_self = is_w & (my_i == other)

    def query_grad(i):
        a0 = dot_tn(sg_s[i, 0], kbd_s[i, 0])
        a1 = dot_tn(sg_s[i, 1], kbd_s[i, 1])
        qg_s[i, :, 0:512] = a0[:, 0:512].astype(BF16)
        qg_s[i, :, 512:WIN] = (a0[:, 512:WIN] + a1[:, 0:CB]).astype(BF16)
        qg_s[i, :, WIN:D] = a1[:, CB:WIN].astype(BF16)

    for i in range(2):
        query_grad(i)
        l_ref[i] = dot_nt(qg_s[i], wq_s[...]).astype(BF16)

    for i in range(2):
        @pl.when(jnp.logical_not(is_w & (my_i == i)))
        def _():
            wait_bytes(slabs_of(NJ), hrecv.at[i])

        hc_s[i] = dot_nt(sel, hid_s[i]).astype(BF16)

    def scatter_sum(n):
        def body(k, c):
            jj = lax.rem(my_j + k, NJ)
            remote(
                part_s.at[n, :, cols(jj)], rs_s.at[n, my_j], rssend.at[n], rsrecv.at[n],
                d, where_worker(my_i * NJ + jj),
            )
            return c

        lax.fori_loop(1, NJ, body, 0)
        rs_s[n, my_j] = part_s[n, :, cols(my_j)]

    def scatter_wait(n):
        wait_bytes(rs_s.at[n, pl.ds(0, NJ - 1)], rsrecv.at[n])
        total = rs_s[n, 0]
        for k in range(1, NJ):
            total = total + rs_s[n, k]
        return total

    @pl.when(is_w)
    def _():
        @pl.when(from_self)
        def _():
            b1_s[chip] = kvb_s[:, cols(my_j)]
            wait_bytes(b1_s.at[pl.ds(0, NS // 2 - 1)], b1recv)

        @pl.when(jnp.logical_not(from_self))
        def _():
            wait_bytes(b1_s, b1recv)

        total = b1_s[0].astype(F32)
        for k in range(1, NS // 2):
            total = total + b1_s[k].astype(F32)
        low = total.astype(BF16)
        part_s[0] = dot_nt(low[0:NP], wc[2]) + dot_nt(low[NP : 2 * NP], wc[3])
        scatter_sum(0)
        eg = scatter_wait(0).astype(BF16)
        part_s[1] = dot_nt(eg, wc[1])
        scatter_sum(1)
        eg_src[...] = eg
        eg_s[my_i, :, cols(my_j)] = eg
        to_plane(eg_src, eg_s.at[my_i, :, cols(my_j)], egsend, egrecv.at[my_i])
        pre = pre_s[...]
        sig = 1.0 / (1.0 + jnp.exp(-pre))
        slope = sig * (1.0 + pre * (1.0 - sig))
        ag = (scatter_wait(1) * slope).astype(BF16)
        ag_src[...] = ag
        ag_s[my_i, :, cols(my_j)] = ag
        to_plane(ag_src, ag_s.at[my_i, :, cols(my_j)], agsend, agrecv.at[my_i])
        part_s[2] = dot_nt(ag, wc[0])
        scatter_sum(2)

    def wait_blocks(sem, i):
        mine = is_w & (my_i == i)

        @pl.when(mine)
        def _():
            wait_bytes(slabs_of(NJ - 1), sem)

        @pl.when(jnp.logical_not(mine))
        def _():
            wait_bytes(slabs_of(NJ), sem)

    eighth = lax.rem(s, NZ)

    def z_scatter(k):
        def body(n, c):
            b = lax.rem(d + n, NZ)
            remote(gz_s.at[k, :, cols(b)], zr_s.at[k, 0, d], zsend.at[k], zrecv.at[k, 0], b, s)
            return c

        lax.fori_loop(1, NZ, body, 0)
        zr_s[k, 0, d] = gz_s[k, :, cols(d)]

        @pl.when(eighth == d)
        def _():
            zr_s[k, 1, d] = gz_s[k, :, NZ * CB : D]

        @pl.when(eighth != d)
        def _():
            remote(gz_s.at[k, :, pl.ds(NZ * CB, CB)], zr_s.at[k, 1, d], zsend.at[k], zrecv.at[k, 1], eighth, s)

    def z_gather(k):
        def reduce(h, b):
            wait_bytes(zr_s.at[k, h, pl.ds(0, NZ - 1)], zrecv.at[k, h])
            total = zr_s[k, h, 0].astype(F32)
            for n in range(1, NZ):
                total = total + zr_s[k, h, n].astype(F32)
            zf_s[k, :, cols(b)] = total.astype(BF16)

            def body(n, c):
                remote(zf_s.at[k, :, cols(b)], zf_s.at[k, :, cols(b)], zasend.at[k, h], zarecv.at[k], lax.rem(d + n, NZ), s)
                return c

            lax.fori_loop(1, NZ, body, 0)

        reduce(0, d)

        @pl.when(eighth == d)
        def _():
            reduce(1, NZ)

    def z_finish(k, out):
        @pl.when(eighth == d)
        def _():
            wait_bytes(zr_s.at[k, 0, pl.ds(0, NZ - 1)], zarecv.at[k])

        @pl.when(eighth != d)
        def _():
            wait_bytes(zr_s.at[k, 0], zarecv.at[k])

        out[...] = zf_s[k].astype(F32)[0:SR]

    for i in range(2):
        wait_blocks(egrecv.at[i], i)
    gz_s[0] = (dot_nn(hc_s[0], eg_s[0]) + dot_nn(hc_s[1], eg_s[1])).astype(BF16)
    z_scatter(0)

    for i in range(2):
        wait_blocks(agrecv.at[i], i)
    gz_s[1] = (dot_nn(pc_s[0], ag_s[0]) + dot_nn(pc_s[1], ag_s[1])).astype(BF16)
    z_scatter(1)

    @pl.when(is_w)
    def _():
        pgsrc_s[...] = scatter_wait(2).astype(BF16)
        pgf_s[my_i, :, cols(my_j)] = pgsrc_s[...]
        to_plane(pgsrc_s, pgf_s.at[my_i, :, cols(my_j)], pgsend, pgrecv.at[my_i])

    z_gather(0)
    z_gather(1)
    z_finish(0, sg_ref)
    for i in range(2):
        wait_blocks(pgrecv.at[i], i)
    pg_ref[...] = pgf_s[...]

    @pl.when(is_w)
    def _():
        for w in range(4):
            wait_bytes(wbuf.at[w, pl.ds(0, 2 * NJ - 1)], wsend.at[w])
        for sem in (hsend.at[0], esend):
            wait_bytes(slabs_of(NJ - 1), sem)
        for n in range(3):
            wait_bytes(rs_s.at[n, pl.ds(0, NJ - 1)], rssend.at[n])
        wait_bytes(wide_s(NS - NJ), hsend.at[1])
        for sem in (egsend, agsend, pgsend):
            wait_bytes(wide_s(NS - 1), sem)

        @pl.when(direct)
        def _():
            wait_bytes(b1_s.at[pl.ds(0, NS // 2 - 1)], kvsend)

        @pl.when(jnp.logical_not(direct))
        def _():
            wait_bytes(b1_s, kvsend)

    @pl.when(jnp.logical_not(is_w))
    def _():
        for w in range(4):
            wait_bytes(wbuf.at[w, pl.ds(0, 2 * NJ)], wsend.at[w])

    @pl.when(from_self)
    def _():
        wait_bytes(b1_s.at[pl.ds(0, NJ - 1)], b1send)

    @pl.when(jnp.logical_not(from_self))
    def _():
        wait_bytes(b1_s.at[pl.ds(0, NJ)], b1send)

    wait_bytes(kv_s.at[core], fwsend)
    wait_bytes(pair_s, prsend)
    for k in range(2):
        @pl.when(eighth == d)
        def _():
            wait_bytes(zr_s.at[k, 0, pl.ds(0, NZ - 1)], zsend.at[k])
            wait_bytes(zr_s.at[k, 0, pl.ds(0, NZ - 1)], zasend.at[k, 1])

        @pl.when(eighth != d)
        def _():
            wait_bytes(zr_s.at[k, 0], zsend.at[k])

        wait_bytes(zr_s.at[k, 0, pl.ds(0, NZ - 1)], zasend.at[k, 0])
    z_finish(1, fg_ref)


def local(
    latents, out_grad, phrases, query_weight, key_weight, value_weight, first_weight, second_weight,
    region_first, region_last, phrase_counts,
):
    vmem = pl.BlockSpec(memory_space=pltpu.VMEM)
    hbm = pl.BlockSpec(memory_space=pltpu.HBM)
    V = pltpu.VMEM
    I32 = jnp.int32
    DMA = pltpu.SemaphoreType.DMA
    scratch = [
        pltpu.SMEM((2, NP), I32), pltpu.SMEM((2, NP), I32), pltpu.SMEM((2,), I32),
        V((2, NP, D), BF16), V((4, SR, D), BF16),
        V((2, TOK, D), BF16), V((2, TOK, D), BF16), V((D, D), BF16), V((2, TOK, D), BF16), V((2, TOK, D), BF16),
        V((4, NS, SR, CB), BF16), V((D, CB), F32), V((4, D, CB), BF16),
        V((NP, CB), BF16), V((2, NP, D), BF16), V((NP, D), BF16), V((2 * NP, CB), BF16), V((2, 2 * NP, D), BF16),
        V((NP, CB), F32),
        V((2, 2, 8 * NP, WIN), BF16), V((8 * NP, WIN), BF16), V((8 * NP, TOK), F32), V((8 * NP, TOK), F32),
        V((8 * NP, TOK), BF16), V((2, 2, 8 * NP, TOK), BF16), V((2, 2 * NP, D), F32), V((2 * NP, D), F32),
        V((2 * NP, D), BF16), V((NS // 2, 2 * NP, CB), BF16), V((3, NP, D), F32), V((3, NJ, NP, CB), F32),
        V((NP, CB), BF16), V((2, NP, D), BF16), V((NP, CB), BF16), V((2, NP, D), BF16), V((NP, CB), BF16),
        V((2, NP, D), BF16),
        V((2, SRP, NP), BF16), V((2, SRP, NP), BF16), V((2, SRP, D), BF16), V((2, 2, NZ, SRP, CB), BF16),
        V((2, SRP, D), BF16),
        DMA((11,)),
        DMA((4,)), DMA((4,)), DMA((2,)), DMA((2,)), DMA(()), DMA(()), DMA(()), DMA(()), DMA(()), DMA(()), DMA(()), DMA(()),
        DMA(()), DMA(()), DMA((3,)), DMA((3,)), DMA(()), DMA((2,)), DMA(()), DMA((2,)), DMA(()), DMA((2,)),
        DMA((2,)), DMA((2, 2)), DMA((2, 2)), DMA((2,)),
    ]
    return pl.pallas_call(
        kernel,
        out_shape=(
            jax.ShapeDtypeStruct((2, TOK, D), BF16),
            jax.ShapeDtypeStruct((2, NP, D), BF16),
            jax.ShapeDtypeStruct((SR, D), F32),
            jax.ShapeDtypeStruct((SR, D), F32),
        ),
        in_specs=[hbm] * 11,
        out_specs=(vmem, vmem, vmem, vmem),
        scratch_shapes=scratch,
        compiler_params=pltpu.CompilerParams(
            collective_id=0, has_side_effects=True, vmem_limit_bytes=48 * 2**20
        ),
    )(
        *[
            pltpu.with_memory_space_constraint(array, pltpu.HBM)
            for array in (
                region_first, region_last, phrase_counts, latents, out_grad, query_weight, phrases,
                first_weight, second_weight, key_weight, value_weight,
            )
        ]
    )


def solution(mesh):
    in_specs = (
        P("dp", "seq", None), P("dp", "seq", None), P("dp", None, None), P(),
        P("seq", None), P("seq", None), P("seq", None), P("seq", None),
        P("dp", None), P("dp", None), P("dp"),
    )
    out_specs = (P("dp", "seq", None), P("dp", None, None), P("seq", None), P("seq", None))
    return jax.shard_map(local, mesh=mesh, in_specs=in_specs, out_specs=out_specs, check_vma=False)
```

time: 107 us -> 83.6 us (0.78)
  Pallas kernels: 94.5 us -> 79.4 us
  local copies, waits for them, and re-layouts: 11.6 us -> 3.41 us
    pallas_call x1, Pallas kernels: 94.5 us -> 79.4 us  [local(): pl.pallas_call(kernel, out_shape=(jax.ShapeDtypeStruct((2, TOK, D), BF16)...]
    unnamed x22 -> x4, local copies, waits for them, and re-layouts: 11.6 us -> 3.41 us
where the time goes in v2:
time: 83.6 us; the launch traced here: 83.4 us
  Pallas kernels  79.4 us (95%)
  local copies, waits for them, and re-layouts  3.41 us (4%)
    pallas_call x1, Pallas kernels, local(): pl.pallas_call(kernel, out_shape=(jax.ShapeDtypeStruct((2, TOK, D), BF16)...  79.4 us
    unnamed x4, local copies, waits for them, and re-layouts  3.41 us

profile of v2, /device:TPU:4, one launch (start us, length us, event | category | flops | bytes accessed | tf_op | source)
XLA Modules:
  0.0 83.4 jit_solution(12318057104794859278)
XLA Ops:
  0.6 79.4 %shard_map.138 = (bf16[2,512,1152]{2,1,0:T(8,128)(2,1)S(1)}, bf16[2,32,1152]{2,1,0:T(8,128)(2,1)S(1)}, f32[36,1152]{1,0:T(8,128)S(1)}, f32[36,1152]{1,0:T(8,128)S(1)}) custom-call(s32[2,32]{1,0:T(2,128)} %first_hbm.1, s32[2,32]{1,0:T(2,128)} %last_hbm.1, s32[2]{0:T(128)} %count_hbm.1, bf16[2,512,1152]{2,1,0:T(8,128)(2,1)} %lat_hbm.1, ...), custom_call_target="tpu_custom_call" | custom-call | tf_op jit(solution)/shard_map/pallas_call | solution.py:565
  80.0 1.4 %copy.19 = bf16[2,512,1152]{2,1,0:T(8,128)(2,1)} copy(bf16[2,512,1152]{2,1,0:T(8,128)(2,1)S(1)} %get-tuple-element.8) | data formatting | bytes 4718592
  81.4 0.7 copy.20
  82.1 0.7 copy.21
  82.8 0.7 copy.22

commit v3 on v2

--- a/solution.py
+++ b/solution.py
@@ -39,27 +39,13 @@
 
 
 def where_worker(n):
-    i, j = n // NJ, lax.rem(n, NJ)
-    k = j // 2
-    y = lax.rem(1 + 2 * i + jnp.where(k == 1, 3, jnp.where(k == 2, 1, 0)), 4)
-    x = lax.rem(1 + 2 * i + jnp.where(k == 3, 3, jnp.where(k == 4, 1, 0)), 4)
-    return (y * 4 + x) * 2 + lax.rem(j, 2)
+    j = lax.rem(n, NJ)
+    return 2 * (4 * (j // 3) + lax.rem(j, 3)) + n // NJ
 
 
 def worker_at(t):
-    y, x, c = t // 8, lax.rem(t // 2, 4), lax.rem(t, 2)
-
-    def block(i):
-        ry, rx = lax.rem(y + 7 - 2 * i, 4), lax.rem(x + 7 - 2 * i, 4)
-        row = jnp.where(rx == 0, 0, jnp.where(rx == 3, 3, jnp.where(rx == 1, 4, 9)))
-        col = jnp.where(ry == 3, 1, jnp.where(ry == 1, 2, 9))
-        k = jnp.where(ry == 0, row, jnp.where(rx == 0, col, 9))
-        return 2 * k + c
-
-    j0, j1 = block(0), block(1)
-    i = jnp.where(j0 < NJ, 0, 1)
-    j = jnp.where(j0 < NJ, j0, j1)
-    return i, j, j < NJ
+    y, x = t // 8, lax.rem(t // 2, 4)
+    return lax.rem(t, 2), 3 * y + x, (x < 3) & (y < 3)
 
 
 def kernel(
@@ -75,7 +61,7 @@
     eg_src, eg_s, ag_src, ag_s, pgsrc_s, pgf_s,
     hc_s, pc_s, gz_s, zr_s, zf_s,
     ld_sem,
-    wsend, wrecv, hsend, hrecv, esend, erecv, kvsend, kvrecv, fwsend, fwrecv, prsend, prrecv,
+    wsend, wrecv, swsend, swrecv, hsend, hrecv, esend, erecv, kvsend, kvrecv, fwsend, fwrecv, prsend, prrecv,
     b1send, b1recv, rssend, rsrecv, egsend, egrecv, agsend, agrecv, pgsend, pgrecv,
     zsend, zrecv, zasend, zarecv,
 ):
@@ -128,19 +114,28 @@
         loads[n].wait()
     pl.semaphore_wait(barrier, NS - 1 + NZ - 1)
 
+    half = NS // 2
+
     def send_weight(w):
         def body(k, c):
-            n = lax.rem(s + k, 2 * NJ)
-            j = lax.rem(n, NJ)
-            t = where_worker(n)
+            j = lax.rem(chip + k, NJ)
+            t = where_worker(core * NJ + j)
 
             @pl.when(t != s)
             def _():
-                remote(w_s.at[w, :, cols(j)], wbuf.at[w, s], wsend.at[w], wrecv.at[w], d, t)
-
-            return c
-
-        lax.fori_loop(0, 2 * NJ, body, 0)
+                remote(w_s.at[w, :, cols(j)], wbuf.at[w, core * half + chip], wsend.at[w], wrecv.at[w], d, t)
+
+            return c
+
+        lax.fori_loop(0, NJ, body, 0)
+
+    def swap_start(w):
+        wait_bytes(wbuf.at[w, pl.ds(0, half - 1)], wrecv.at[w])
+        got = wbuf.at[w, pl.ds(core * half, half)]
+        remote(got, got, swsend.at[w], swrecv.at[w], d, mate)
+
+    def swap_wait(w):
+        wait_bytes(wbuf.at[w, pl.ds(0, half)], swrecv.at[w])
 
     send_weight(0)
     send_weight(1)
@@ -148,7 +143,7 @@
     @pl.when(is_w)
     def _():
         for w in range(4):
-            wbuf[w, s] = w_s[w, :, cols(my_j)]
+            wbuf[w, core * half + chip] = w_s[w, :, cols(my_j)]
 
     loads[6].wait()
     sel = (
@@ -167,7 +162,7 @@
 
     def compact(w):
         for p in range(NS):
-            w_f32[p * SR : (p + 1) * SR, :] = wbuf[w, p].astype(F32)
+            w_f32[p * SR : (p + 1) * SR, :] = wbuf[w, (p % 2) * half + p // 2].astype(F32)
         wc[w] = w_f32[...].astype(BF16)
 
     def to_co_workers(src, dst, ssem, rsem):
@@ -193,7 +188,8 @@
 
     @pl.when(is_w)
     def _():
-        wait_bytes(wbuf.at[0, pl.ds(0, NS - 1)], wrecv.at[0])
+        swap_start(0)
+        swap_wait(0)
         compact(0)
         pre = dot_nn(phr_ref[my_i], wc[0])
         pre_s[...] = pre
@@ -203,14 +199,17 @@
         to_co_workers(hid_src, hid_s.at[my_i, :, cols(my_j)], hsend.at[0], hrecv.at[my_i])
         send_weight(2)
         send_weight(3)
-        wait_bytes(wbuf.at[1, pl.ds(0, NS - 1)], wrecv.at[1])
+        swap_start(1)
+        swap_wait(1)
         compact(1)
         wait_bytes(slabs_of(NJ - 1), hrecv.at[my_i])
         enc = dot_nn(hid_s[my_i], wc[1]).astype(BF16)
         enc_s[:, cols(my_j)] = enc
         to_co_workers(enc_s.at[:, cols(my_j)], enc_s.at[:, cols(my_j)], esend, erecv)
         for w in (2, 3):
-            wait_bytes(wbuf.at[w, pl.ds(0, NS - 1)], wrecv.at[w])
+            swap_start(w)
+        for w in (2, 3):
+            swap_wait(w)
             compact(w)
         wait_bytes(slabs_of(NJ - 1), erecv)
         enc_all = enc_s[...]
@@ -304,11 +303,11 @@
 
     @pl.when(direct)
     def _():
-        wait_bytes(b1_s.at[pl.ds(0, NJ - 1)], kvrecv)
+        wait_bytes(b1_s.at[pl.ds(0, NJ - 1), pl.ds(0, NP)], kvrecv)
 
     @pl.when(jnp.logical_not(direct))
     def _():
-        wait_bytes(b1_s.at[pl.ds(0, NJ)], kvrecv)
+        wait_bytes(b1_s.at[pl.ds(0, NJ), pl.ds(0, NP)], kvrecv)
 
     remote(kv_s.at[core], kv_s.at[core], fwsend, fwrecv, d, mate)
     attention(core)
@@ -316,7 +315,7 @@
     wait_bytes(kv_s.at[other], fwrecv)
     attention(other)
     wait_bytes(pair_s, prrecv)
-    kvb_s[...] = (kvp_s[other] + pair_s[...]).astype(BF16)
+    kvb_s[...] = kvp_s[other] + pair_s[...]
 
     def send_part(k, c):
         jj = lax.rem(chip + k, NJ)
@@ -379,9 +378,9 @@
         def _():
             wait_bytes(b1_s, b1recv)
 
-        total = b1_s[0].astype(F32)
+        total = b1_s[0]
         for k in range(1, NS // 2):
-            total = total + b1_s[k].astype(F32)
+            total = total + b1_s[k]
         low = total.astype(BF16)
         part_s[0] = dot_nt(low[0:NP], wc[2]) + dot_nt(low[NP : 2 * NP], wc[3])
         scatter_sum(0)
@@ -488,7 +487,8 @@
     @pl.when(is_w)
     def _():
         for w in range(4):
-            wait_bytes(wbuf.at[w, pl.ds(0, 2 * NJ - 1)], wsend.at[w])
+            wait_bytes(wbuf.at[w, pl.ds(0, NJ - 1)], wsend.at[w])
+            wait_bytes(wbuf.at[w, pl.ds(0, half)], swsend.at[w])
         for sem in (hsend.at[0], esend):
             wait_bytes(slabs_of(NJ - 1), sem)
         for n in range(3):
@@ -499,16 +499,16 @@
 
         @pl.when(direct)
         def _():
-            wait_bytes(b1_s.at[pl.ds(0, NS // 2 - 1)], kvsend)
+            wait_bytes(b1_s.at[pl.ds(0, NS // 2 - 1), pl.ds(0, NP)], kvsend)
 
         @pl.when(jnp.logical_not(direct))
         def _():
-            wait_bytes(b1_s, kvsend)
+            wait_bytes(b1_s.at[:, pl.ds(0, NP)], kvsend)
 
     @pl.when(jnp.logical_not(is_w))
     def _():
         for w in range(4):
-            wait_bytes(wbuf.at[w, pl.ds(0, 2 * NJ)], wsend.at[w])
+            wait_bytes(wbuf.at[w, pl.ds(0, NJ)], wsend.at[w])
 
     @pl.when(from_self)
     def _():
@@ -552,13 +552,13 @@
         V((NP, CB), F32),
         V((2, 2, 8 * NP, WIN), BF16), V((8 * NP, WIN), BF16), V((8 * NP, TOK), F32), V((8 * NP, TOK), F32),
         V((8 * NP, TOK), BF16), V((2, 2, 8 * NP, TOK), BF16), V((2, 2 * NP, D), F32), V((2 * NP, D), F32),
-        V((2 * NP, D), BF16), V((NS // 2, 2 * NP, CB), BF16), V((3, NP, D), F32), V((3, NJ, NP, CB), F32),
+        V((2 * NP, D), F32), V((NS // 2, 2 * NP, CB), F32), V((3, NP, D), F32), V((3, NJ, NP, CB), F32),
         V((NP, CB), BF16), V((2, NP, D), BF16), V((NP, CB), BF16), V((2, NP, D), BF16), V((NP, CB), BF16),
         V((2, NP, D), BF16),
         V((2, SRP, NP), BF16), V((2, SRP, NP), BF16), V((2, SRP, D), BF16), V((2, 2, NZ, SRP, CB), BF16),
         V((2, SRP, D), BF16),
         DMA((11,)),
-        DMA((4,)), DMA((4,)), DMA((2,)), DMA((2,)), DMA(()), DMA(()), DMA(()), DMA(()), DMA(()), DMA(()), DMA(()), DMA(()),
+        DMA((4,)), DMA((4,)), DMA((4,)), DMA((4,)), DMA((2,)), DMA((2,)), DMA(()), DMA(()), DMA(()), DMA(()), DMA(()), DMA(()), DMA(()), DMA(()),
         DMA(()), DMA(()), DMA((3,)), DMA((3,)), DMA(()), DMA((2,)), DMA(()), DMA((2,)), DMA(()), DMA((2,)),
         DMA((2,)), DMA((2, 2)), DMA((2, 2)), DMA((2,)),
     ]

time: 83.6 us -> 82.7 us (0.989)
  no operation moved by 1% of the time
where the time goes in v3:
time: 82.7 us; the launch traced here: 82.6 us
  Pallas kernels  78.6 us (95%)
  local copies, waits for them, and re-layouts  3.41 us (4%)
    pallas_call x1, Pallas kernels, local(): pl.pallas_call(kernel, out_shape=(jax.ShapeDtypeStruct((2, TOK, D), BF16)...  78.6 us
    unnamed x4, local copies, waits for them, and re-layouts  3.41 us

profile of v3, /device:TPU:4, one launch (start us, length us, event | category | flops | bytes accessed | tf_op | source)
XLA Modules:
  0.0 82.6 jit_solution(16746201088701658928)
XLA Ops:
  0.6 78.6 %shard_map.138 = (bf16[2,512,1152]{2,1,0:T(8,128)(2,1)S(1)}, bf16[2,32,1152]{2,1,0:T(8,128)(2,1)S(1)}, f32[36,1152]{1,0:T(8,128)S(1)}, f32[36,1152]{1,0:T(8,128)S(1)}) custom-call(s32[2,32]{1,0:T(2,128)} %first_hbm.1, s32[2,32]{1,0:T(2,128)} %last_hbm.1, s32[2]{0:T(128)} %count_hbm.1, bf16[2,512,1152]{2,1,0:T(8,128)(2,1)} %lat_hbm.1, ...), custom_call_target="tpu_custom_call" | custom-call | tf_op jit(solution)/shard_map/pallas_call | solution.py:565
  79.2 1.4 %copy.19 = bf16[2,512,1152]{2,1,0:T(8,128)(2,1)} copy(bf16[2,512,1152]{2,1,0:T(8,128)(2,1)S(1)} %get-tuple-element.8) | data formatting | bytes 4718592
  80.6 0.7 copy.20
  81.3 0.7 copy.21
  81.9 0.7 copy.22

commit v4 on v3

--- a/solution.py
+++ b/solution.py
@@ -51,7 +51,7 @@
 def kernel(
     first_hbm, last_hbm, count_hbm,
     lat_hbm, og_hbm, wq_hbm, phr_hbm, w1_hbm, w2_hbm, wk_hbm, wv_hbm,
-    l_ref, pg_ref, fg_ref, sg_ref,
+    l_ref, pg_ref, zf_s,
     first_ref, last_ref, count_ref, phr_ref, w_s,
     x_s, g_s, wq_s, q_s, qg_s,
     wbuf, w_f32, wc,
@@ -59,7 +59,7 @@
     kbd_s, vbd_s, st_s, pt_s, pr_s, sg_s, kvp_s, pair_s,
     kvb_s, b1_s, part_s, rs_s,
     eg_src, eg_s, ag_src, ag_s, pgsrc_s, pgf_s,
-    hc_s, pc_s, gz_s, zr_s, zf_s,
+    hc_s, pc_s, gz_s, zr_s,
     ld_sem,
     wsend, wrecv, swsend, swrecv, hsend, hrecv, esend, erecv, kvsend, kvrecv, fwsend, fwrecv, prsend, prrecv,
     b1send, b1recv, rssend, rsrecv, egsend, egrecv, agsend, agrecv, pgsend, pgrecv,
@@ -450,7 +450,7 @@
         def _():
             reduce(1, NZ)
 
-    def z_finish(k, out):
+    def z_finish(k):
         @pl.when(eighth == d)
         def _():
             wait_bytes(zr_s.at[k, 0, pl.ds(0, NZ - 1)], zarecv.at[k])
@@ -459,7 +459,6 @@
         def _():
             wait_bytes(zr_s.at[k, 0], zarecv.at[k])
 
-        out[...] = zf_s[k].astype(F32)[0:SR]
 
     for i in range(2):
         wait_blocks(egrecv.at[i], i)
@@ -479,7 +478,7 @@
 
     z_gather(0)
     z_gather(1)
-    z_finish(0, sg_ref)
+    z_finish(0)
     for i in range(2):
         wait_blocks(pgrecv.at[i], i)
     pg_ref[...] = pgf_s[...]
@@ -531,7 +530,7 @@
             wait_bytes(zr_s.at[k, 0], zsend.at[k])
 
         wait_bytes(zr_s.at[k, 0, pl.ds(0, NZ - 1)], zasend.at[k, 0])
-    z_finish(1, fg_ref)
+    z_finish(1)
 
 
 def local(
@@ -556,22 +555,20 @@
         V((NP, CB), BF16), V((2, NP, D), BF16), V((NP, CB), BF16), V((2, NP, D), BF16), V((NP, CB), BF16),
         V((2, NP, D), BF16),
         V((2, SRP, NP), BF16), V((2, SRP, NP), BF16), V((2, SRP, D), BF16), V((2, 2, NZ, SRP, CB), BF16),
-        V((2, SRP, D), BF16),
         DMA((11,)),
         DMA((4,)), DMA((4,)), DMA((4,)), DMA((4,)), DMA((2,)), DMA((2,)), DMA(()), DMA(()), DMA(()), DMA(()), DMA(()), DMA(()), DMA(()), DMA(()),
         DMA(()), DMA(()), DMA((3,)), DMA((3,)), DMA(()), DMA((2,)), DMA(()), DMA((2,)), DMA(()), DMA((2,)),
         DMA((2,)), DMA((2, 2)), DMA((2, 2)), DMA((2,)),
     ]
-    return pl.pallas_call(
+    latent_grad, phrase_grad, sums = pl.pallas_call(
         kernel,
         out_shape=(
             jax.ShapeDtypeStruct((2, TOK, D), BF16),
             jax.ShapeDtypeStruct((2, NP, D), BF16),
-            jax.ShapeDtypeStruct((SR, D), F32),
-            jax.ShapeDtypeStruct((SR, D), F32),
+            jax.ShapeDtypeStruct((2, SRP, D), BF16),
         ),
         in_specs=[hbm] * 11,
-        out_specs=(vmem, vmem, vmem, vmem),
+        out_specs=(vmem, vmem, vmem),
         scratch_shapes=scratch,
         compiler_params=pltpu.CompilerParams(
             collective_id=0, has_side_effects=True, vmem_limit_bytes=48 * 2**20
@@ -585,6 +582,7 @@
             )
         ]
     )
+    return latent_grad, phrase_grad, sums[1, 0:SR].astype(F32), sums[0, 0:SR].astype(F32)
 
 
 def solution(mesh):

time: 82.7 us -> 82.2 us (level)
  local copies, waits for them, and re-layouts: 3.41 us -> 2.07 us
    unnamed x4 -> x2, local copies, waits for them, and re-layouts: 3.41 us -> 2.07 us
where the time goes in v4:
time: 82.2 us; the launch traced here: 82.1 us
  Pallas kernels  78.6 us (96%)
  local copies, waits for them, and re-layouts  2.07 us (3%)
    pallas_call x1, Pallas kernels, local(): pl.pallas_call(kernel, out_shape=(jax.ShapeDtypeStruct((2, TOK, D), BF16)...  78.6 us
    unnamed x2, local copies, waits for them, and re-layouts  2.07 us

profile of v4, /device:TPU:4, one launch (start us, length us, event | category | flops | bytes accessed | tf_op | source)
XLA Modules:
  0.0 82.1 jit_solution(9736677731028390556)
XLA Ops:
  0.6 78.6 %shard_map.138 = (bf16[2,512,1152]{2,1,0:T(8,128)(2,1)S(1)}, bf16[2,32,1152]{2,1,0:T(8,128)(2,1)S(1)}, bf16[2,40,1152]{2,1,0:T(8,128)(2,1)S(1)}) custom-call(s32[2,32]{1,0:T(2,128)} %first_hbm.1, s32[2,32]{1,0:T(2,128)} %last_hbm.1, s32[2]{0:T(128)} %count_hbm.1, bf16[2,512,1152]{2,1,0:T(8,128)(2,1)} %lat_hbm.1, bf16[2,512,1152]{2,1,0:T(8,128)(2,1)} %og_hbm.1, ...), custom_call_target="tpu_custom_call" | custom-call | tf_op jit(solution)/shard_map/pallas_call | solution.py:563
  79.3 0.8 bitcast_convert_fusion
  80.0 1.4 %copy.17 = bf16[2,512,1152]{2,1,0:T(8,128)(2,1)} copy(bf16[2,512,1152]{2,1,0:T(8,128)(2,1)S(1)} %get-tuple-element.16) | data formatting | bytes 4718592
  81.4 0.7 copy.18
